TPU v7x, 128 devices: a whole 4x4x4 slice. The times are simulated.
128 devices in a mesh: mem: 8 (over x, core), tile: 16 (over z, y).
Axes of the slice: x: 4, y: 4, z: 4, core: 2. Of those that a mesh axis runs over, the one named last changes fastest.
Arguments:
- members: bfloat16 [16, 137, 8192], P('mem', None, 'tile'), may hold values from -18 to 18
- vertical: bfloat16 [137, 137], replicated, may hold values from 0 to 1, as said below
- jacobian: bfloat16 [2048, 231, 137], P('tile'), may hold values from -0.5 to 0.5
- sketch_bits: int32 [3, 2048, 231], P(None, 'tile'), may hold values from 0 to 1
- test_bits: int32 [3, 2048, 231], P(None, 'tile'), may hold values from 0 to 1
- obs_column: int32 [2048], P('tile'), may hold values from 0 to 8191, as said below
- obs_slot: int32 [2048], P('tile'), may hold values from 0 to 31, as said below
Outputs:
- image_q: float32 [3, 2048, 231], P(None, 'tile')
- image_w: float32 [3, 2048, 231], P(None, 'tile')
- trace_mean: float32 [], replicated
- sketch_rayleigh: float32 [], replicated
Inputs may be any that keep to these rules, and one draw needn't show every extreme that they name: The observations of owner d are rows d * 128 to (d + 1) * 128 - 1; an observation's column lies in tile obs_column // 512. `obs_slot`: among one owner's observations whose columns lie in the same tile the slots are distinct, so at most 32 of them lie in one tile; every owner has exactly 32 observations in some tile. A vertical correlation matrix: symmetric, positive semidefinite, with ones on the diagonal.
All inputs are finite; a program needn't handle non-finite values.
Results may differ from a plain program's by a relative error of at most 0.0053.
Values may be sent and summed in bfloat16 or wider, within the bound.
No kernel may reach another device: no remote copies, remote signals or barrier semaphores. Data moves between devices by JAX's collectives and lax.ppermute only.
A program may use at most 128 MiB of HBM per device.

v0:
```python
import jax
import jax.numpy as jnp
from jax import lax
from jax.sharding import Mesh
from jax.sharding import PartitionSpec as P

CB = 32
K = 3
STEPS = 6
TILE = ("tile_0", "tile_1")
diffusion_rate = 0.2
highest = lax.Precision.HIGHEST


def with_halo(block, sides, width):
    for axis, dim in sides:
        count = lax.axis_size(axis)
        forward = [(i, i + 1) for i in range(count - 1)]
        forward.append((count - 1, 0))
        backward = [(target, source) for source, target in forward]
        low = lax.ppermute(
            lax.slice_in_dim(block, block.shape[dim] - width, None, axis=dim), axis, forward
        )
        high = lax.ppermute(lax.slice_in_dim(block, 0, width, axis=dim), axis, backward)
        block = jnp.concatenate([low, block, high], axis=dim)
    return block


def gather_turned(arrays, axis, dims):
    turned = [jnp.moveaxis(a, dim, 0) for a, dim in zip(arrays, dims)]
    widths = [t[0].size for t in turned]
    both = jnp.concatenate([t.reshape(-1, w) for t, w in zip(turned, widths)], axis=1)
    whole = lax.all_gather(both, axis, axis=0, tiled=True)
    pieces = jnp.split(whole, [sum(widths[:k]) for k in range(1, len(widths))], axis=1)
    return tuple(
        (
            jnp.moveaxis(b.reshape(-1, *t.shape[1:]), 0, dim)
            for b, t, dim in zip(pieces, turned, dims)
        )
    )


def split_up(value, dim, peers):
    before, after = (value.shape[:dim], value.shape[dim + 1 :])
    return jnp.moveaxis(value.reshape(*before, peers, -1, *after), dim, 0)


def sum_at_owner(value, axis, dim):
    pieces = split_up(value, dim, lax.axis_size(axis))
    arrived = lax.all_to_all(pieces, axis, split_axis=0, concat_axis=0, tiled=True)
    return arrived.sum(axis=0)


def from_everyone(value, axis):
    peers = lax.axis_size(axis)
    return lax.all_to_all(
        jnp.broadcast_to(value[None], (peers, *value.shape)), axis, 0, 0, tiled=True
    )


def joined_along(pieces, dim):
    lengths = list(pieces.shape[1:])
    lengths[dim] *= pieces.shape[0]
    return jnp.moveaxis(pieces, 0, dim).reshape(lengths)


def collect_2(value, axis, dim):
    pieces = from_everyone(value, axis)
    return joined_along(pieces, dim)


def by_axis(value, axes):
    for axis in axes:
        value = lax.psum(value, axis)
    return value


def relax(extended):
    length = extended.shape[-1] - 2 * CB
    center = extended[..., CB : CB + length]
    places = jnp.arange(length) % CB
    west_ok = (places > 0).astype(jnp.float32)
    east_ok = (places < CB - 1).astype(jnp.float32)
    north = extended[..., :length]
    south = extended[..., 2 * CB :]
    west = extended[..., CB - 1 : CB - 1 + length]
    east = extended[..., CB + 1 : CB + 1 + length]
    return center + diffusion_rate * (
        north - center + (south - center) + west_ok * (west - center) + east_ok * (east - center)
    )


def diffuse(state):
    extended = with_halo(state, ((TILE, 2),), STEPS * CB)
    for _ in range(STEPS):
        extended = relax(extended)
    return extended


def on_device(members, vertical, jacobian, sketch_bits, test_bits, obs_column, obs_slot):
    tile_count = lax.axis_size(TILE)
    my_tile = lax.axis_index(TILE)
    obs_local = obs_column.shape[0]
    levels = members.shape[1]
    cell_count = members.shape[2]
    channels = jacobian.shape[1]
    capacity = obs_local // 4
    slot_count = tile_count * capacity
    ensemble = members.shape[0] * lax.axis_size("mem")
    count = float(obs_local * tile_count * channels)
    all_columns, all_slots = gather_turned((obs_column, obs_slot), TILE, (0, 0))
    owners = jnp.arange(tile_count * obs_local, dtype=jnp.int32) // obs_local
    target = jnp.where(
        all_columns // cell_count == my_tile, owners * capacity + all_slots, slot_count
    )
    cell_table = (
        jnp.zeros((slot_count,), jnp.int32).at[target].set(all_columns % cell_count, mode="drop")
    )
    occupied = jnp.zeros((slot_count,), jnp.bool_).at[target].set(True, mode="drop")
    spread = ((cell_table[:, None] == jnp.arange(cell_count)[None, :]) & occupied[:, None]).astype(
        jnp.bfloat16
    )
    my_positions = obs_column // cell_count * capacity + obs_slot
    collect = (my_positions[:, None] == jnp.arange(slot_count)[None, :]).astype(jnp.bfloat16)

    def apply_operator(vectors):
        probes = vectors.shape[0]
        rows = probes * levels
        adjoint = jnp.einsum(
            "ocl,poc->plo",
            jacobian,
            vectors.astype(jnp.bfloat16),
            preferred_element_type=jnp.float32,
        ).astype(jnp.bfloat16)
        outgoing = jnp.dot(
            adjoint.reshape(rows, obs_local), collect, preferred_element_type=jnp.float32
        ).astype(jnp.bfloat16)
        arrived = lax.all_to_all(outgoing, TILE, split_axis=1, concat_axis=1, tiled=True)
        field_sum = jnp.dot(arrived, spread, preferred_element_type=jnp.float32).reshape(
            probes, levels, cell_count
        )

        def member_step(number, carry):
            member = lax.dynamic_index_in_dim(members, number, 0, keepdims=False).astype(
                jnp.float32
            )
            product = (member[None] * field_sum).astype(jnp.bfloat16)
            mixed = jnp.einsum("kl,plc->pkc", vertical, product, preferred_element_type=jnp.float32)
            return carry + member[None] * diffuse(mixed)

        partial_sum = lax.fori_loop(
            0, members.shape[0], member_step, jnp.zeros((probes, levels, cell_count), jnp.float32)
        )
        partial_cols = jnp.take(partial_sum.reshape(rows, cell_count), cell_table, axis=1).reshape(
            rows, tile_count, capacity
        )
        picked = sum_at_owner(partial_cols, "mem", 2) / (ensemble - 1)
        outbound = picked.astype(jnp.bfloat16)
        returned = lax.all_to_all(outbound, TILE, split_axis=1, concat_axis=1, tiled=True)
        returned = collect_2(returned, "mem", 2)
        returned = returned.reshape(rows, slot_count)
        profile = jnp.dot(returned, collect.T, preferred_element_type=jnp.float32).astype(
            jnp.bfloat16
        )
        profile = profile.reshape(probes, levels, obs_local)
        return jnp.einsum("ocl,plo->poc", jacobian, profile, preferred_element_type=jnp.float32)

    sketch = (2 * sketch_bits - 1).astype(jnp.float32)
    test = (2 * test_bits - 1).astype(jnp.float32)
    sketch_image = apply_operator(sketch)
    products = by_axis(
        jnp.einsum("ioc,joc->ij", sketch_image, sketch_image, precision=highest), TILE
    )
    lower = jnp.linalg.cholesky(products)
    inverse_lower = lax.linalg.triangular_solve(
        lower, jnp.eye(K, dtype=jnp.float32), left_side=True, lower=True
    )
    basis = jnp.sqrt(count) * jnp.einsum(
        "ji,ioc->joc", inverse_lower, sketch_image, precision=highest
    )
    intersection = by_axis(jnp.einsum("ioc,joc->ij", basis, test, precision=highest), TILE) / count
    remainder = test - jnp.einsum("ij,ioc->joc", intersection, basis, precision=highest)
    images = apply_operator(jnp.concatenate([basis, remainder], axis=0))
    image_q = images[:K]
    image_w = images[K:]
    trace_q, trace_w = (
        by_axis(jnp.sum(basis * image_q), TILE),
        by_axis(jnp.sum(remainder * image_w), TILE),
    )
    trace_mean = trace_q / (count * count) + trace_w / (K * count)
    sketch_rayleigh = trace_q / (K * count)
    return (image_q, image_w, trace_mean, sketch_rayleigh)


def solution(mesh):
    finer = Mesh(mesh.devices.reshape(mesh.shape["mem"], 4, 4), ("mem", "tile_0", "tile_1"))
    return jax.shard_map(
        on_device,
        mesh=finer,
        in_specs=(
            P("mem", None, TILE),
            P(),
            P(TILE, None, None),
            P(None, TILE, None),
            P(None, TILE, None),
            P(TILE),
            P(TILE),
        ),
        out_specs=(P(None, TILE, None), P(None, TILE, None), P(), P()),
        check_vma=False,
    )
```

profile of v0, /device:TPU:0, one launch (start us, length us, event | category | flops | bytes accessed | tf_op | source)
XLA Modules:
  0.0 431.1 jit_solution(6855449706677383312)
XLA Ops:
  0.6 13.3 %copy.96 = bf16[128,231,137]{1,2,0:T(8,128)(2,1)} copy(bf16[128,231,137]{0,1,2:T(8,128)(2,1)} %param.13) | data formatting | bytes 16203264 | tf_op args[2]
  14.2 6.2 %fusion.179 = bf16[3,137,128]{1,0,2:T(4,128)(2,1)S(1)} fusion(bf16[3,128,231]{2,0,1:T(4,128)(2,1)S(1)} %copy.95, bf16[128,231,137]{1,2,0:T(8,128)(2,1)} %copy.96), kind=kOutput, calls=%fused_computation.270 | convolution fusion | flops 24357504 | bytes 8384256 | tf_op jit(solution)/shard_map/ocl,poc->plo/dot_general | solution.py:129
  22.1 8.2 %all-to-all-start = ((bf16[411,16,32]{0,2,1:T(8,128)(2,1)}), bf16[411,16,32]{0,2,1:T(8,128)(2,1)S(1)}, u32[]{:S(2)}, u32[]{:S(2)}) async-start(bf16[411,16,32]{0,2,1:T(8,128)(2,1)} %bitcast.5), calls=%async_computation | async-start | bytes 1048576 | tf_op jit(solution)/shard_map/all_to_all | solution.py:138
  30.2 25.7 %all_gather.3 = s32[2048,2]{0,1:T(2,128)S(1)} all-gather(s32[128,2]{0,1:T(2,128)S(1)} %pad_add_fusion), channel_id=1, replica_groups=mesh['mem'=8,'tile_0'=4,'tile_1'=4] {'tile_0','tile_1'}, dimensions={0}, use_global_device_ids=true | all-gather | bytes 17408 | tf_op jit(solution)/shard_map/all_gather | solution.py:33
  56.1 8.0 %scatter_custom_fusion = s32[512]{0:T(512)S(1)} fusion(s32[2048]{0:T(1024)S(1)} %bitcast.110, s32[2048]{0:T(1024)S(1)} %add_select_fusion.12, s32[]{:T(128)} %constant.386.clone.1), kind=kCustom, calls=%fused_computation.340 | custom fusion | bytes 2052 | tf_op jit(solution)/shard_map/scatter | solution.py:117
  64.3 9.1 %scatter_custom_fusion.1 = pred[512]{0:T(512)(128)(4,1)S(1)} fusion(s32[2048]{0:T(1024)S(1)} %bitcast.111, pred[2048]{0:T(1024)(128)(4,1)S(1)} %broadcast.1456, pred[]{:T(512)} %constant.400.clone.1), kind=kCustom, calls=%fused_computation.342 | custom fusion | bytes 513 | tf_op jit(solution)/shard_map/scatter | solution.py:119
  75.1 1.9 fusion.183
  77.0 49.0 %while.32 = (s32[]{:T(128)}, f32[3,137,512]{2,1,0:T(8,128)S(1)}, bf16[2,137,512]{2,1,0:T(8,128)(2,1)S(1)}, f32[3,137,512]{2,1,0:T(8,128)S(1)}, bf16[137,137]{1,0:T(8,128)(2,1)S(1)}, /*index=5*/s32[]{:T(128)}, s32[]{:T(128)}) while((s32[]{:T(128)}, f32[3,137,512]{2,1,0:T(8,128)S(1)}, bf16[2,137,512]{2,1,0:T(8,128)(2,1)S(1)}, ...), condition=%wide.region_3.4_spmd.clone, body=%wide.region_2.3_spmd.clone.sunk | while | flops 77786176 | bytes 52359552 | solution.py:151
  78.9 2.1 collective-permute-start
  81.0 6.5 %collective-permute-done = f32[3,137,192]{2,1,0:T(8,128)} collective-permute-done((f32[3,137,192]{2,1,0:T(8,128)}, f32[3,137,192]{2,1,0:T(8,128)}, u32[]{:S(2)}, u32[]{:S(2)}) %collective-permute-start) | collective-permute-done | bytes 315680 | tf_op jit(solution)/shard_map/while/body/eval_jaxpr/ppermute | solution.py:24
  87.5 5.2 %collective-permute-done.1 = f32[3,137,192]{2,1,0:T(8,128)} collective-permute-done((f32[3,137,192]{2,1,0:T(8,128)S(1)}, f32[3,137,192]{2,1,0:T(8,128)}, u32[]{:S(2)}, u32[]{:S(2)}) %collective-permute-start.1) | collective-permute-done | bytes 315680 | tf_op jit(solution)/shard_map/while/body/eval_jaxpr/ppermute | solution.py:21
  92.7 1.6 pad_maximum_fusion.5
  94.3 1.7 fusion.266
  104.5 1.8 collective-permute-start.1
  106.4 6.5 %collective-permute-done = f32[3,137,192]{2,1,0:T(8,128)} collective-permute-done((f32[3,137,192]{2,1,0:T(8,128)}, f32[3,137,192]{2,1,0:T(8,128)}, u32[]{:S(2)}, u32[]{:S(2)}) %collective-permute-start) | collective-permute-done | bytes 315680 | tf_op jit(solution)/shard_map/while/body/eval_jaxpr/ppermute | solution.py:24
  112.9 3.3 collective-permute-done.1
  117.9 1.7 fusion.266
  127.1 1.6 gather_fusion
  129.5 20.5 %all_to_all.48 = f32[8,411,16,4]{1,3,2,0:T(4,128)S(1)} all-to-all(f32[8,411,16,4]{1,3,2,0:T(4,128)S(1)} %copy.102), channel_id=1, replica_groups=mesh['mem'=8,'tile_0'=4,'tile_1'=4] {'mem'}, dimensions={0} | all-to-all | bytes 1683456 | tf_op jit(solution)/shard_map/all_to_all | solution.py:50
  150.3 10.2 %all_to_all.49 = bf16[411,16,4]{0,2,1:T(4,128)(2,1)S(1)} all-to-all(bf16[411,16,4]{0,2,1:T(4,128)(2,1)S(1)} %multiply_convert_fusion.5), channel_id=1, replica_groups=mesh['mem'=8,'tile_0'=4,'tile_1'=4] {'tile_0','tile_1'}, dimensions={1} | all-to-all | bytes 105216 | tf_op jit(solution)/shard_map/all_to_all | solution.py:159
  160.6 12.8 %all_to_all.50 = bf16[8,411,16,4]{1,3,2,0:T(4,128)(2,1)S(1)} all-to-all(bf16[8,411,16,4]{1,3,2,0:T(4,128)(2,1)S(1)} %broadcast_in_dim.146), channel_id=1, replica_groups=mesh['mem'=8,'tile_0'=4,'tile_1'=4] {'mem'}, dimensions={0} | all-to-all | bytes 841728 | tf_op jit(solution)/shard_map/all_to_all | solution.py:56
  174.5 5.0 %convolution_bitcast_fusion.2 = f32[3,128,231]{2,0,1:T(4,128)S(1)} fusion(bf16[3,137,128]{1,0,2:T(4,128)(2,1)S(1)} %copy.104, bf16[128,231,137]{1,2,0:T(8,128)(2,1)} %copy.96), kind=kOutput, calls=%fused_computation.267 | convolution fusion | flops 24304896 | bytes 8561664 | tf_op jit(solution)/shard_map/ocl,plo->poc/dot_general | solution.py:166
  179.6 2.3 convolution_bitcast_fusion.5
  182.0 8.8 %psum.56 = f32[3,3]{0,1:T(4,128)S(1)} all-reduce(f32[3,3]{0,1:T(4,128)S(1)} %convolution_bitcast_fusion.5), channel_id=1, replica_groups=mesh['mem'=8,'tile_0'=4,'tile_1'=4] {'tile_0'}, use_global_device_ids=true, to_apply=%region_5.6 | all-reduce | flops 9 | bytes 72 | tf_op jit(solution)/shard_map/psum | solution.py:74
  191.1 8.9 %psum.57 = f32[3,3]{0,1:T(4,128)S(1)} all-reduce(f32[3,3]{0,1:T(4,128)S(1)} %psum.56), channel_id=1, replica_groups=mesh['mem'=8,'tile_0'=4,'tile_1'=4] {'tile_1'}, use_global_device_ids=true, to_apply=%region_6.7 | all-reduce | flops 9 | bytes 72 | tf_op jit(solution)/shard_map/psum | solution.py:74
  203.2 2.2 convolution_bitcast_fusion.3
  205.4 8.6 %psum.58 = f32[3,3]{1,0:T(4,128)S(1)} all-reduce(f32[3,3]{1,0:T(4,128)S(1)} %convolution_bitcast_fusion.3), channel_id=1, replica_groups=mesh['mem'=8,'tile_0'=4,'tile_1'=4] {'tile_0'}, use_global_device_ids=true, to_apply=%region_9.10 | all-reduce | flops 9 | bytes 72 | tf_op jit(solution)/shard_map/psum | solution.py:74
  214.0 8.6 %psum.59 = f32[3,3]{1,0:T(4,128)S(1)} all-reduce(f32[3,3]{1,0:T(4,128)S(1)} %psum.58), channel_id=1, replica_groups=mesh['mem'=8,'tile_0'=4,'tile_1'=4] {'tile_1'}, use_global_device_ids=true, to_apply=%region_10.11 | all-reduce | flops 9 | bytes 72 | tf_op jit(solution)/shard_map/psum | solution.py:74
  224.3 6.2 %fusion.178 = bf16[6,137,128]{1,0,2:T(8,128)(2,1)S(1)} fusion(bf16[6,128,231]{2,0,1:T(8,128)(2,1)S(1)} %copy.116, bf16[128,231,137]{1,2,0:T(8,128)(2,1)} %copy.96), kind=kOutput, calls=%fused_computation.266 | convolution fusion | flops 48715008 | bytes 8666880 | tf_op jit(solution)/shard_map/ocl,poc->plo/dot_general | solution.py:129
  232.7 3.6 all-to-all-start.4
  236.3 12.4 %all-to-all-done.4 = bf16[822,16,32]{0,2,1:T(8,128)(2,1)S(1)} async-done(((bf16[822,16,32]{0,2,1:T(8,128)(2,1)}), bf16[822,16,32]{0,2,1:T(8,128)(2,1)S(1)}, u32[]{:S(2)}, u32[]{:S(2)}) %all-to-all-start.4) | async-done | bytes 841760 | tf_op jit(solution)/shard_map/all_to_all | solution.py:138
  248.7 3.1 dot_general.78
  251.8 3.8 fusion.176
  255.6 79.9 %while.33 = (s32[]{:T(128)}, f32[6,137,512]{2,1,0:T(8,128)}, bf16[2,137,512]{2,1,0:T(8,128)(2,1)S(1)}, f32[6,137,512]{2,1,0:T(8,128)}, bf16[137,137]{1,0:T(8,128)(2,1)S(1)}, /*index=5*/s32[]{:T(128)}, s32[]{:T(128)}) while((s32[]{:T(128)}, f32[6,137,512]{2,1,0:T(8,128)}, bf16[2,137,512]{2,1,0:T(8,128)(2,1)S(1)}, ...), condition=%wide.region_12.13_spmd.clone, body=%wide.region_11.12_spmd.clone.sunk | while | flops 155461888 | bytes 112613240 | solution.py:151
  255.8 2.0 convolution_bitcast_fusion.9
  261.1 11.3 %collective-permute-done.2 = f32[6,137,192]{2,1,0:T(8,128)} collective-permute-done((f32[6,137,192]{2,1,0:T(8,128)}, f32[6,137,192]{2,1,0:T(8,128)}, u32[]{:S(2)}, u32[]{:S(2)}) %collective-permute-start.2) | collective-permute-done | bytes 631328 | tf_op jit(solution)/shard_map/while/body/eval_jaxpr/ppermute | solution.py:24
  272.4 4.3 collective-permute-done.3
  276.7 2.3 pad_maximum_fusion.6
  279.0 3.4 fusion.280
  282.4 2.8 fusion.282
  285.2 2.8 fusion.284
  288.0 2.3 fusion.286
  290.4 2.3 fusion.288
  292.7 2.1 fusion.290
  296.1 2.0 convolution_bitcast_fusion.9
  299.5 1.8 collective-permute-start.3
  301.4 11.3 %collective-permute-done.2 = f32[6,137,192]{2,1,0:T(8,128)} collective-permute-done((f32[6,137,192]{2,1,0:T(8,128)}, f32[6,137,192]{2,1,0:T(8,128)}, u32[]{:S(2)}, u32[]{:S(2)}) %collective-permute-start.2) | collective-permute-done | bytes 631328 | tf_op jit(solution)/shard_map/while/body/eval_jaxpr/ppermute | solution.py:24
  312.7 3.3 collective-permute-done.3
  316.0 2.3 pad_maximum_fusion.6
  318.3 3.4 fusion.280
  321.7 2.8 fusion.282
  324.5 2.8 fusion.284
  327.3 2.3 fusion.286
  329.6 2.3 fusion.288
  332.0 2.1 fusion.290
  335.5 1.8 reshape.300
  338.1 2.6 gather_fusion.1
  340.7 1.8 gather.15
  343.3 26.8 %all_to_all.51 = f32[8,822,16,4]{1,3,2,0:T(4,128)S(1)} all-to-all(f32[8,822,16,4]{1,3,2,0:T(4,128)S(1)} %copy.123), channel_id=1, replica_groups=mesh['mem'=8,'tile_0'=4,'tile_1'=4] {'mem'}, dimensions={0} | all-to-all | bytes 3366912 | tf_op jit(solution)/shard_map/all_to_all | solution.py:50
  370.6 10.5 %all_to_all.52 = bf16[822,16,4]{0,2,1:T(4,128)(2,1)S(1)} all-to-all(bf16[822,16,4]{0,2,1:T(4,128)(2,1)S(1)} %multiply_convert_fusion.4), channel_id=1, replica_groups=mesh['mem'=8,'tile_0'=4,'tile_1'=4] {'tile_0','tile_1'}, dimensions={1} | all-to-all | bytes 210432 | tf_op jit(solution)/shard_map/all_to_all | solution.py:159
  381.4 17.0 %all_to_all.53 = bf16[8,822,16,4]{1,3,2,0:T(4,128)(2,1)S(1)} all-to-all(bf16[8,822,16,4]{1,3,2,0:T(4,128)(2,1)S(1)} %broadcast_in_dim.148), channel_id=1, replica_groups=mesh['mem'=8,'tile_0'=4,'tile_1'=4] {'mem'}, dimensions={0} | all-to-all | bytes 1683456 | tf_op jit(solution)/shard_map/all_to_all | solution.py:56
  400.1 5.0 %fusion.218 = f32[128,6,231]{2,1,0:T(8,128)S(1)} fusion(bf16[6,137,128]{1,0,2:T(8,128)(2,1)S(1)} %copy.125, bf16[128,231,137]{1,2,0:T(8,128)(2,1)} %copy.96), kind=kOutput, calls=%fused_computation.351 | convolution fusion | flops 48609792 | bytes 9021696 | tf_op jit(solution)/shard_map/ocl,plo->poc/dot_general | solution.py:166
  407.9 9.2 %all-reduce.1 = (f32[]{:T(128)}, f32[]{:T(128)}) all-reduce(f32[]{:T(128)} %get-tuple-element.418, f32[]{:T(128)} %get-tuple-element.384), channel_id=1, replica_groups=mesh['mem'=8,'tile_0'=4,'tile_1'=4] {'tile_0'}, use_global_device_ids=true, to_apply=%region_15.16 | all-reduce | flops 2 | bytes 16 | tf_op jit(solution)/shard_map/psum | solution.py:74
  417.1 9.6 %all-reduce = (f32[]{:T(128)}, f32[]{:T(128)}) all-reduce(f32[]{:T(128)} %get-tuple-element.382, f32[]{:T(128)} %get-tuple-element.383), channel_id=1, replica_groups=mesh['mem'=8,'tile_0'=4,'tile_1'=4] {'tile_1'}, use_global_device_ids=true, to_apply=%region_16.17 | all-reduce | flops 2 | bytes 16 | tf_op jit(solution)/shard_map/psum | solution.py:74
  (168 shorter events, 46.6 us)
Async XLA Ops:
  0.6 13.3 %copy-start.13 = (s32[3,128,231]{1,2,0:T(8,128)S(1)}, s32[3,128,231]{1,2,0:T(8,128)}, u32[]{:S(2)}) copy-start(s32[3,128,231]{1,2,0:T(8,128)} %param.14) | copy-start | bytes 1064452
  14.2 6.4 %copy-start.21 = (s32[128]{0:T(128)S(1)}, s32[128]{0:T(128)}, u32[]{:S(2)}) copy-start(s32[128]{0:T(128)} %param.17) | copy-start | bytes 1540
  14.2 6.4 %copy-start.22 = (s32[128]{0:T(128)S(1)}, s32[128]{0:T(128)}, u32[]{:S(2)}) copy-start(s32[128]{0:T(128)} %param.16) | copy-start | bytes 1540
  20.4 43.7 %copy-start.14 = (bf16[2,137,512]{2,0,1:T(2,128)(2,1)S(1)}, bf16[2,137,512]{2,0,1:T(2,128)(2,1)}, u32[]{:S(2)}) copy-start(bf16[2,137,512]{2,0,1:T(2,128)(2,1)} %param.11) | copy-start | bytes 841732
  20.7 210.2 %copy-start.19 = (s32[128]{0:T(128)}, s32[128]{0:T(128)S(1)}, u32[]{:S(2)}) copy-start(s32[128]{0:T(128)S(1)} %multiply_add_fusion) | copy-start | bytes 1540
  22.1 51.5 %all-to-all-start = ((bf16[411,16,32]{0,2,1:T(8,128)(2,1)}), bf16[411,16,32]{0,2,1:T(8,128)(2,1)S(1)}, u32[]{:S(2)}, u32[]{:S(2)}) async-start(bf16[411,16,32]{0,2,1:T(8,128)(2,1)} %bitcast.5), calls=%async_computation | async-start | bytes 1048576 | tf_op jit(solution)/shard_map/all_to_all | solution.py:138
  64.3 64.8 %copy-start.15 = (pred[16,8,4]{2,1,0:T(8,128)(4,1)}, pred[16,8,4]{2,1,0:T(8,128)(4,1)S(1)}, u32[]{:S(2)}) copy-start(pred[16,8,4]{2,1,0:T(8,128)(4,1)S(1)} %broadcast_in_dim.137) | copy-start | bytes 1540
  73.5 53.6 %copy-start.17 = (s32[1024]{0:T(1024)}, s32[1024]{0:T(1024)S(1)}, u32[]{:S(2)}) copy-start(s32[1024]{0:T(1024)S(1)} %pad_clamp_fusion) | copy-start | bytes 12292
  73.5 3.5 copy-start.8
  77.0 0.7 copy-start.2
  78.9 8.6 %collective-permute-start = (f32[3,137,192]{2,1,0:T(8,128)}, f32[3,137,192]{2,1,0:T(8,128)}, u32[]{:S(2)}, u32[]{:S(2)}) collective-permute-start(f32[3,137,192]{2,1,0:T(8,128)} %get-tuple-element.507), channel_id=1, source_target_pairs={{1,0},{2,1},{3,2},{4,3},{5,4},{6,5},{7,6},{8,7},{9,8},{10,9},{11,1... | collective-permute-start | bytes 946952 | tf_op jit(solution)/shard_map/while/body/eval_jaxpr/ppermute | solution.py:24
  81.0 11.7 %collective-permute-start.1 = (f32[3,137,192]{2,1,0:T(8,128)S(1)}, f32[3,137,192]{2,1,0:T(8,128)}, u32[]{:S(2)}, u32[]{:S(2)}) collective-permute-start(f32[3,137,192]{2,1,0:T(8,128)S(1)} %get-tuple-element.508), channel_id=1, source_target_pairs={{0,1},{1,2},{2,3},{3,4},{4,5},{5,6},{6,7},{7,8},{8,9},{9,10},{10,1... | collective-permute-start | bytes 946952 | tf_op jit(solution)/shard_map/while/body/eval_jaxpr/ppermute | solution.py:21
  101.3 1.1 copy-start.3
  102.4 0.7 copy-start.2
  104.3 8.6 %collective-permute-start = (f32[3,137,192]{2,1,0:T(8,128)}, f32[3,137,192]{2,1,0:T(8,128)}, u32[]{:S(2)}, u32[]{:S(2)}) collective-permute-start(f32[3,137,192]{2,1,0:T(8,128)} %get-tuple-element.507), channel_id=1, source_target_pairs={{1,0},{2,1},{3,2},{4,3},{5,4},{6,5},{7,6},{8,7},{9,8},{10,9},{11,1... | collective-permute-start | bytes 946952 | tf_op jit(solution)/shard_map/while/body/eval_jaxpr/ppermute | solution.py:24
  104.5 11.7 %collective-permute-start.1 = (f32[3,137,192]{2,1,0:T(8,128)S(1)}, f32[3,137,192]{2,1,0:T(8,128)}, u32[]{:S(2)}, u32[]{:S(2)}) collective-permute-start(f32[3,137,192]{2,1,0:T(8,128)S(1)} %get-tuple-element.508), channel_id=1, source_target_pairs={{0,1},{1,2},{2,3},{3,4},{4,5},{5,6},{6,7},{7,8},{8,9},{9,10},{10,1... | collective-permute-start | bytes 946952 | tf_op jit(solution)/shard_map/while/body/eval_jaxpr/ppermute | solution.py:21
  124.8 1.1 copy-start.3
  125.9 0.7 copy-start.4
  174.5 7.4 %copy-start.11 = (s32[3,128,231]{1,2,0:T(8,128)S(1)}, s32[3,128,231]{1,2,0:T(8,128)}, u32[]{:S(2)}) copy-start(s32[3,128,231]{1,2,0:T(8,128)} %param.15) | copy-start | bytes 1064452
  203.2 20.7 %copy-start.6 = (f32[3,128,231]{1,2,0:T(8,128)}, f32[3,128,231]{1,2,0:T(8,128)S(1)}, u32[]{:S(2)}) copy-start(f32[3,128,231]{1,2,0:T(8,128)S(1)} %get-tuple-element.389) | copy-start | bytes 1064452
  223.7 6.8 %copy-start.9 = (f32[3,128,231]{1,0,2:T(4,128)}, f32[3,128,231]{1,0,2:T(4,128)S(1)}, u32[]{:S(2)}) copy-start(f32[3,128,231]{1,0,2:T(4,128)S(1)} %fusion.190) | copy-start | bytes 1064452
  232.7 16.1 %all-to-all-start.4 = ((bf16[822,16,32]{0,2,1:T(8,128)(2,1)}), bf16[822,16,32]{0,2,1:T(8,128)(2,1)S(1)}, u32[]{:S(2)}, u32[]{:S(2)}) async-start(bf16[822,16,32]{0,2,1:T(8,128)(2,1)} %bitcast.19), calls=%async_computation.4 | async-start | bytes 1835008 | tf_op jit(solution)/shard_map/all_to_all | solution.py:138
  251.8 3.8 copy-start.5
  259.0 13.4 %collective-permute-start.2 = (f32[6,137,192]{2,1,0:T(8,128)}, f32[6,137,192]{2,1,0:T(8,128)}, u32[]{:S(2)}, u32[]{:S(2)}) collective-permute-start(f32[6,137,192]{2,1,0:T(8,128)} %get-tuple-element.526), channel_id=1, source_target_pairs={{1,0},{2,1},{3,2},{4,3},{5,4},{6,5},{7,6},{8,7},{9,8},{10,9},{11,1... | collective-permute-start | bytes 1893896 | tf_op jit(solution)/shard_map/while/body/eval_jaxpr/ppermute | solution.py:24
  260.2 16.5 %collective-permute-start.3 = (f32[6,137,192]{2,1,0:T(8,128)S(1)}, f32[6,137,192]{2,1,0:T(8,128)}, u32[]{:S(2)}, u32[]{:S(2)}) collective-permute-start(f32[6,137,192]{2,1,0:T(8,128)S(1)} %get-tuple-element.527), channel_id=1, source_target_pairs={{0,1},{1,2},{2,3},{3,4},{4,5},{5,6},{6,7},{7,8},{8,9},{9,10},{10,1... | collective-permute-start | bytes 1893896 | tf_op jit(solution)/shard_map/while/body/eval_jaxpr/ppermute | solution.py:21
  290.4 2.4 copy-start
  294.8 1.2 copy-start.1
  299.3 13.4 %collective-permute-start.2 = (f32[6,137,192]{2,1,0:T(8,128)}, f32[6,137,192]{2,1,0:T(8,128)}, u32[]{:S(2)}, u32[]{:S(2)}) collective-permute-start(f32[6,137,192]{2,1,0:T(8,128)} %get-tuple-element.526), channel_id=1, source_target_pairs={{1,0},{2,1},{3,2},{4,3},{5,4},{6,5},{7,6},{8,7},{9,8},{10,9},{11,1... | collective-permute-start | bytes 1893896 | tf_op jit(solution)/shard_map/while/body/eval_jaxpr/ppermute | solution.py:24
  299.5 16.5 %collective-permute-start.3 = (f32[6,137,192]{2,1,0:T(8,128)S(1)}, f32[6,137,192]{2,1,0:T(8,128)}, u32[]{:S(2)}, u32[]{:S(2)}) collective-permute-start(f32[6,137,192]{2,1,0:T(8,128)S(1)} %get-tuple-element.527), channel_id=1, source_target_pairs={{0,1},{1,2},{2,3},{3,4},{4,5},{5,6},{6,7},{7,8},{8,9},{9,10},{10,1... | collective-permute-start | bytes 1893896 | tf_op jit(solution)/shard_map/while/body/eval_jaxpr/ppermute | solution.py:21
  329.6 2.4 copy-start
  334.1 1.2 copy-start.1
  337.3 0.8 copy-start.18
  340.7 1.9 copy-start.16
  398.3 0.8 copy-start.20
  405.1 1.0 copy-start.7
  405.1 1.1 copy-start.10
  405.1 1.2 copy-start.12
where the time goes:
time: 439 us; the launch traced here: 431 us
  blocking collectives  177 us (40%)
  waiting for transfers between devices  64.1 us (15%)
  local copies, waits for them, and re-layouts  61.2 us (14%)
  other arithmetic  60.9 us (14%)
  matrix products  41.2 us (9%)
  starting transfers between devices  19.9 us (5%)
  between operations  5.68 us (1%)
    psum x6, blocking collectives, by_axis(): value = lax.psum(value, axis)  53.8 us
    all_to_all x2, blocking collectives, sum_at_owner(): lax.all_to_all(pieces, axis, split_axis=0, concat_axis=0, tiled=True)  47.3 us
    add x20, other arithmetic, relax(): center + diffusion_rate * (north - center + (south - center) + west_ok *...  41.3 us
    ppermute x4, waiting for transfers between devices, with_halo(): lax.ppermute(lax.slice_in_dim(block, 0, width, axis=dim), axis, backward)  35.6 us
    all_to_all x2, blocking collectives, from_everyone(): lax.all_to_all(jnp.broadcast_to(value[None], (peers, *value.shape)), axis...  29.7 us
    all_gather x1, blocking collectives, gather_turned(): whole = lax.all_gather(both, axis, axis=0, tiled=True)  25.7 us
    all_to_all x2, blocking collectives, apply_operator(): lax.all_to_all(outbound, TILE, split_axis=1, concat_axis=1, tiled=True)  20.7 us
    ppermute x4, waiting for transfers between devices, with_halo(): lax.ppermute(lax.slice_in_dim(block, block.shape[dim] - width, None, axis...  16.1 us
  transfers between devices with their start and end apart: 10, of which 9 were waited for; matrix products, arithmetic and copies ran while one was open for 4% of the time, Pallas kernels for 0%

commit v1 on v0

--- a/solution.py
+++ b/solution.py
@@ -135,7 +135,10 @@
         outgoing = jnp.dot(
             adjoint.reshape(rows, obs_local), collect, preferred_element_type=jnp.float32
         ).astype(jnp.bfloat16)
-        arrived = lax.all_to_all(outgoing, TILE, split_axis=1, concat_axis=1, tiled=True)
+        arrived = jnp.concatenate(
+            lax.all_to_all(jnp.stack(jnp.split(outgoing, lax.axis_size(TILE), axis=1)), TILE, 0, 0),
+            axis=1,
+        )
         field_sum = jnp.dot(arrived, spread, preferred_element_type=jnp.float32).reshape(
             probes, levels, cell_count
         )

time: 439 us -> 464 us (1.057)
  local copies, waits for them, and re-layouts: 61.2 us -> 85.2 us
    unnamed x40 -> x70, local copies, waits for them, and re-layouts: 15 us -> 33.4 us
    another operation x0 -> x36, local copies, waits for them, and re-layouts: none -> 7.55 us  [apply_operator(): jnp.stack(jnp.split(outgoing, lax.axis_size(TILE), axis=1))]
where the time goes in v1:
time: 464 us; the launch traced here: 455 us
  blocking collectives  177 us (38%)
  local copies, waits for them, and re-layouts  85.2 us (18%)
  waiting for transfers between devices  64.1 us (14%)
  other arithmetic  60.9 us (13%)
  matrix products  41.2 us (9%)
  starting transfers between devices  19.9 us (4%)
  between operations  5.84 us (1%)
    psum x6, blocking collectives, by_axis(): value = lax.psum(value, axis)  53.8 us
    all_to_all x2, blocking collectives, sum_at_owner(): lax.all_to_all(pieces, axis, split_axis=0, concat_axis=0, tiled=True)  47.1 us
    add x20, other arithmetic, relax(): center + diffusion_rate * (north - center + (south - center) + west_ok *...  41.3 us
    ppermute x4, waiting for transfers between devices, with_halo(): lax.ppermute(lax.slice_in_dim(block, 0, width, axis=dim), axis, backward)  35.6 us
    unnamed x70, local copies, waits for them, and re-layouts  33.4 us
    all_to_all x2, blocking collectives, from_everyone(): lax.all_to_all(jnp.broadcast_to(value[None], (peers, *value.shape)), axis...  29.7 us
    all_gather x1, blocking collectives, gather_turned(): whole = lax.all_gather(both, axis, axis=0, tiled=True)  25.7 us
    all_to_all x2, blocking collectives, apply_operator(): lax.all_to_all(outbound, TILE, split_axis=1, concat_axis=1, tiled=True)  20.7 us
  transfers between devices with their start and end apart: 10, of which 9 were waited for; matrix products, arithmetic and copies ran while one was open for 4% of the time, Pallas kernels for 0%

profile of v1, /device:TPU:0, one launch (start us, length us, event | category | flops | bytes accessed | tf_op | source)
XLA Modules:
  0.0 455.2 jit_solution(17265314785735336314)
XLA Ops:
  0.6 13.2 %copy.126 = bf16[128,231,137]{1,2,0:T(8,128)(2,1)} copy(bf16[128,231,137]{0,1,2:T(8,128)(2,1)} %param.13) | data formatting | bytes 16203264 | tf_op args[2]
  14.1 6.2 %fusion.179 = bf16[3,137,128]{1,0,2:T(4,128)(2,1)S(1)} fusion(bf16[3,128,231]{2,0,1:T(4,128)(2,1)S(1)} %copy.125, bf16[128,231,137]{1,2,0:T(8,128)(2,1)} %copy.126), kind=kOutput, calls=%fused_computation.270 | convolution fusion | flops 24357504 | bytes 8384256 | tf_op jit(solution)/shard_map/ocl,poc->plo/dot_general | solution.py:129
  32.7 8.2 %all-to-all-start = ((bf16[16,411,32]{1,2,0:T(8,128)(2,1)}), bf16[16,411,32]{1,2,0:T(8,128)(2,1)S(1)}, u32[]{:S(2)}, u32[]{:S(2)}) async-start(bf16[16,411,32]{1,2,0:T(8,128)(2,1)} %constant_dynamic-update-slice_fusion), calls=%async_computation | async-start | bytes 1048576 | tf_op jit(solution)/shard_map/all_to_all | solution.py:139
  40.9 25.7 %all_gather.3 = s32[2048,2]{0,1:T(2,128)S(1)} all-gather(s32[128,2]{0,1:T(2,128)S(1)} %pad_add_fusion), channel_id=1, replica_groups=mesh['mem'=8,'tile_0'=4,'tile_1'=4] {'tile_0','tile_1'}, dimensions={0}, use_global_device_ids=true | all-gather | bytes 17408 | tf_op jit(solution)/shard_map/all_gather | solution.py:33
  66.7 8.0 %scatter_custom_fusion = s32[512]{0:T(512)S(1)} fusion(s32[2048]{0:T(1024)S(1)} %bitcast.176, s32[2048]{0:T(1024)S(1)} %add_select_fusion.12, s32[]{:T(128)} %constant.386.clone.1), kind=kCustom, calls=%fused_computation.404 | custom fusion | bytes 2052 | tf_op jit(solution)/shard_map/scatter | solution.py:117
  75.0 9.1 %scatter_custom_fusion.1 = pred[512]{0:T(512)(128)(4,1)S(1)} fusion(s32[2048]{0:T(1024)S(1)} %bitcast.177, pred[2048]{0:T(1024)(128)(4,1)S(1)} %broadcast.1456, pred[]{:T(512)} %constant.400.clone.1), kind=kCustom, calls=%fused_computation.406 | custom fusion | bytes 513 | tf_op jit(solution)/shard_map/scatter | solution.py:119
  84.1 1.9 dot_general.68
  86.0 1.9 fusion.183
  87.9 49.0 %while.32 = (s32[]{:T(128)}, f32[3,137,512]{2,1,0:T(8,128)S(1)}, bf16[2,137,512]{2,1,0:T(8,128)(2,1)S(1)}, f32[3,137,512]{2,1,0:T(8,128)S(1)}, bf16[137,137]{1,0:T(8,128)(2,1)S(1)}, /*index=5*/s32[]{:T(128)}, s32[]{:T(128)}) while((s32[]{:T(128)}, f32[3,137,512]{2,1,0:T(8,128)S(1)}, bf16[2,137,512]{2,1,0:T(8,128)(2,1)S(1)}, ...), condition=%wide.region_3.4_spmd.clone, body=%wide.region_2.3_spmd.clone.sunk | while | flops 77786176 | bytes 52359552 | solution.py:154
  89.8 2.1 collective-permute-start
  91.9 6.5 %collective-permute-done = f32[3,137,192]{2,1,0:T(8,128)} collective-permute-done((f32[3,137,192]{2,1,0:T(8,128)}, f32[3,137,192]{2,1,0:T(8,128)}, u32[]{:S(2)}, u32[]{:S(2)}) %collective-permute-start) | collective-permute-done | bytes 315680 | tf_op jit(solution)/shard_map/while/body/eval_jaxpr/ppermute | solution.py:24
  98.4 5.2 %collective-permute-done.1 = f32[3,137,192]{2,1,0:T(8,128)} collective-permute-done((f32[3,137,192]{2,1,0:T(8,128)S(1)}, f32[3,137,192]{2,1,0:T(8,128)}, u32[]{:S(2)}, u32[]{:S(2)}) %collective-permute-start.1) | collective-permute-done | bytes 315680 | tf_op jit(solution)/shard_map/while/body/eval_jaxpr/ppermute | solution.py:21
  105.2 1.7 fusion.266
  115.4 1.8 collective-permute-start.1
  117.3 6.5 %collective-permute-done = f32[3,137,192]{2,1,0:T(8,128)} collective-permute-done((f32[3,137,192]{2,1,0:T(8,128)}, f32[3,137,192]{2,1,0:T(8,128)}, u32[]{:S(2)}, u32[]{:S(2)}) %collective-permute-start) | collective-permute-done | bytes 315680 | tf_op jit(solution)/shard_map/while/body/eval_jaxpr/ppermute | solution.py:24
  123.8 3.3 collective-permute-done.1
  128.8 1.7 fusion.266
  138.0 1.6 gather_fusion
  140.4 20.2 %all_to_all.40 = f32[8,411,16,4]{1,3,2,0:T(4,128)S(1)} all-to-all(f32[8,411,16,4]{1,3,2,0:T(4,128)S(1)} %copy.147), channel_id=1, replica_groups=mesh['mem'=8,'tile_0'=4,'tile_1'=4] {'mem'}, dimensions={0} | all-to-all | bytes 1683456 | tf_op jit(solution)/shard_map/all_to_all | solution.py:50
  160.9 10.2 %all_to_all.41 = bf16[411,16,4]{0,2,1:T(4,128)(2,1)S(1)} all-to-all(bf16[411,16,4]{0,2,1:T(4,128)(2,1)S(1)} %multiply_convert_fusion.5), channel_id=1, replica_groups=mesh['mem'=8,'tile_0'=4,'tile_1'=4] {'tile_0','tile_1'}, dimensions={1} | all-to-all | bytes 105216 | tf_op jit(solution)/shard_map/all_to_all | solution.py:162
  171.3 12.8 %all_to_all.42 = bf16[8,411,16,4]{1,3,2,0:T(4,128)(2,1)S(1)} all-to-all(bf16[8,411,16,4]{1,3,2,0:T(4,128)(2,1)S(1)} %broadcast_in_dim.146), channel_id=1, replica_groups=mesh['mem'=8,'tile_0'=4,'tile_1'=4] {'mem'}, dimensions={0} | all-to-all | bytes 841728 | tf_op jit(solution)/shard_map/all_to_all | solution.py:56
  185.2 5.0 %convolution_bitcast_fusion.2 = f32[3,128,231]{2,0,1:T(4,128)S(1)} fusion(bf16[3,137,128]{1,0,2:T(4,128)(2,1)S(1)} %copy.149, bf16[128,231,137]{1,2,0:T(8,128)(2,1)} %copy.126), kind=kOutput, calls=%fused_computation.267 | convolution fusion | flops 24304896 | bytes 8561664 | tf_op jit(solution)/shard_map/ocl,plo->poc/dot_general | solution.py:169
  190.2 2.3 convolution_bitcast_fusion.5
  192.7 8.8 %psum.56 = f32[3,3]{0,1:T(4,128)S(1)} all-reduce(f32[3,3]{0,1:T(4,128)S(1)} %convolution_bitcast_fusion.5), channel_id=1, replica_groups=mesh['mem'=8,'tile_0'=4,'tile_1'=4] {'tile_0'}, use_global_device_ids=true, to_apply=%region_5.6 | all-reduce | flops 9 | bytes 72 | tf_op jit(solution)/shard_map/psum | solution.py:74
  201.8 8.9 %psum.57 = f32[3,3]{0,1:T(4,128)S(1)} all-reduce(f32[3,3]{0,1:T(4,128)S(1)} %psum.56), channel_id=1, replica_groups=mesh['mem'=8,'tile_0'=4,'tile_1'=4] {'tile_1'}, use_global_device_ids=true, to_apply=%region_6.7 | all-reduce | flops 9 | bytes 72 | tf_op jit(solution)/shard_map/psum | solution.py:74
  213.9 2.2 convolution_bitcast_fusion.3
  216.1 8.6 %psum.58 = f32[3,3]{1,0:T(4,128)S(1)} all-reduce(f32[3,3]{1,0:T(4,128)S(1)} %convolution_bitcast_fusion.3), channel_id=1, replica_groups=mesh['mem'=8,'tile_0'=4,'tile_1'=4] {'tile_0'}, use_global_device_ids=true, to_apply=%region_9.10 | all-reduce | flops 9 | bytes 72 | tf_op jit(solution)/shard_map/psum | solution.py:74
  224.7 8.6 %psum.59 = f32[3,3]{1,0:T(4,128)S(1)} all-reduce(f32[3,3]{1,0:T(4,128)S(1)} %psum.58), channel_id=1, replica_groups=mesh['mem'=8,'tile_0'=4,'tile_1'=4] {'tile_1'}, use_global_device_ids=true, to_apply=%region_10.11 | all-reduce | flops 9 | bytes 72 | tf_op jit(solution)/shard_map/psum | solution.py:74
  235.0 6.2 %fusion.178 = bf16[6,137,128]{1,0,2:T(8,128)(2,1)S(1)} fusion(bf16[6,128,231]{2,0,1:T(8,128)(2,1)S(1)} %copy.161, bf16[128,231,137]{1,2,0:T(8,128)(2,1)} %copy.126), kind=kOutput, calls=%fused_computation.266 | convolution fusion | flops 48715008 | bytes 8666880 | tf_op jit(solution)/shard_map/ocl,poc->plo/dot_general | solution.py:129
  256.6 3.6 all-to-all-start.4
  260.3 12.4 %all-to-all-done.4 = bf16[16,822,32]{1,2,0:T(8,128)(2,1)S(1)} async-done(((bf16[16,822,32]{1,2,0:T(8,128)(2,1)}), bf16[16,822,32]{1,2,0:T(8,128)(2,1)S(1)}, u32[]{:S(2)}, u32[]{:S(2)}) %all-to-all-start.4) | async-done | bytes 841760 | tf_op jit(solution)/shard_map/all_to_all | solution.py:139
  272.7 3.0 dot_general.78
  275.8 3.8 fusion.176
  279.6 80.0 %while.33 = (s32[]{:T(128)}, f32[6,137,512]{2,1,0:T(8,128)}, bf16[2,137,512]{2,1,0:T(8,128)(2,1)S(1)}, f32[6,137,512]{2,1,0:T(8,128)}, bf16[137,137]{1,0:T(8,128)(2,1)S(1)}, /*index=5*/s32[]{:T(128)}, s32[]{:T(128)}) while((s32[]{:T(128)}, f32[6,137,512]{2,1,0:T(8,128)}, bf16[2,137,512]{2,1,0:T(8,128)(2,1)S(1)}, ...), condition=%wide.region_12.13_spmd.clone, body=%wide.region_11.12_spmd.clone.sunk | while | flops 155461888 | bytes 112613240 | solution.py:154
  280.0 2.0 convolution_bitcast_fusion.9
  285.3 11.3 %collective-permute-done.2 = f32[6,137,192]{2,1,0:T(8,128)} collective-permute-done((f32[6,137,192]{2,1,0:T(8,128)}, f32[6,137,192]{2,1,0:T(8,128)}, u32[]{:S(2)}, u32[]{:S(2)}) %collective-permute-start.2) | collective-permute-done | bytes 631328 | tf_op jit(solution)/shard_map/while/body/eval_jaxpr/ppermute | solution.py:24
  296.6 4.3 collective-permute-done.3
  300.9 2.3 pad_maximum_fusion.6
  303.2 3.4 fusion.280
  306.6 2.8 fusion.282
  309.4 2.8 fusion.284
  312.2 2.3 fusion.286
  314.5 2.3 fusion.288
  316.9 2.1 fusion.290
  320.3 2.0 convolution_bitcast_fusion.9
  323.7 1.8 collective-permute-start.3
  325.5 11.3 %collective-permute-done.2 = f32[6,137,192]{2,1,0:T(8,128)} collective-permute-done((f32[6,137,192]{2,1,0:T(8,128)}, f32[6,137,192]{2,1,0:T(8,128)}, u32[]{:S(2)}, u32[]{:S(2)}) %collective-permute-start.2) | collective-permute-done | bytes 631328 | tf_op jit(solution)/shard_map/while/body/eval_jaxpr/ppermute | solution.py:24
  336.8 3.3 collective-permute-done.3
  340.1 2.3 pad_maximum_fusion.6
  342.4 3.4 fusion.280
  345.8 2.8 fusion.282
  348.6 2.8 fusion.284
  351.4 2.3 fusion.286
  353.8 2.3 fusion.288
  356.2 2.1 fusion.290
  359.7 1.8 reshape.306
  362.2 2.7 gather_fusion.1
  364.9 1.8 gather.15
  367.5 26.8 %all_to_all.43 = f32[8,822,16,4]{1,3,2,0:T(4,128)S(1)} all-to-all(f32[8,822,16,4]{1,3,2,0:T(4,128)S(1)} %copy.183), channel_id=1, replica_groups=mesh['mem'=8,'tile_0'=4,'tile_1'=4] {'mem'}, dimensions={0} | all-to-all | bytes 3366912 | tf_op jit(solution)/shard_map/all_to_all | solution.py:50
  394.8 10.5 %all_to_all.44 = bf16[822,16,4]{0,2,1:T(4,128)(2,1)S(1)} all-to-all(bf16[822,16,4]{0,2,1:T(4,128)(2,1)S(1)} %multiply_convert_fusion.4), channel_id=1, replica_groups=mesh['mem'=8,'tile_0'=4,'tile_1'=4] {'tile_0','tile_1'}, dimensions={1} | all-to-all | bytes 210432 | tf_op jit(solution)/shard_map/all_to_all | solution.py:162
  405.5 17.0 %all_to_all.45 = bf16[8,822,16,4]{1,3,2,0:T(4,128)(2,1)S(1)} all-to-all(bf16[8,822,16,4]{1,3,2,0:T(4,128)(2,1)S(1)} %broadcast_in_dim.148), channel_id=1, replica_groups=mesh['mem'=8,'tile_0'=4,'tile_1'=4] {'mem'}, dimensions={0} | all-to-all | bytes 1683456 | tf_op jit(solution)/shard_map/all_to_all | solution.py:56
  424.2 5.0 %fusion.218 = f32[128,6,231]{2,1,0:T(8,128)S(1)} fusion(bf16[6,137,128]{1,0,2:T(8,128)(2,1)S(1)} %copy.185, bf16[128,231,137]{1,2,0:T(8,128)(2,1)} %copy.126), kind=kOutput, calls=%fused_computation.415 | convolution fusion | flops 48609792 | bytes 9021696 | tf_op jit(solution)/shard_map/ocl,plo->poc/dot_general | solution.py:169
  432.0 9.2 %all-reduce.1 = (f32[]{:T(128)}, f32[]{:T(128)}) all-reduce(f32[]{:T(128)} %get-tuple-element.434, f32[]{:T(128)} %get-tuple-element.384), channel_id=1, replica_groups=mesh['mem'=8,'tile_0'=4,'tile_1'=4] {'tile_0'}, use_global_device_ids=true, to_apply=%region_15.16 | all-reduce | flops 2 | bytes 16 | tf_op jit(solution)/shard_map/psum | solution.py:74
  441.3 9.6 %all-reduce = (f32[]{:T(128)}, f32[]{:T(128)}) all-reduce(f32[]{:T(128)} %get-tuple-element.382, f32[]{:T(128)} %get-tuple-element.383), channel_id=1, replica_groups=mesh['mem'=8,'tile_0'=4,'tile_1'=4] {'tile_1'}, use_global_device_ids=true, to_apply=%region_16.17 | all-reduce | flops 2 | bytes 16 | tf_op jit(solution)/shard_map/psum | solution.py:74
  (232 shorter events, 70.4 us)
Async XLA Ops:
  0.6 13.2 %copy-start.13 = (s32[3,128,231]{1,2,0:T(8,128)S(1)}, s32[3,128,231]{1,2,0:T(8,128)}, u32[]{:S(2)}) copy-start(s32[3,128,231]{1,2,0:T(8,128)} %param.14) | copy-start | bytes 1064452
  14.1 6.4 %copy-start.21 = (s32[128]{0:T(128)S(1)}, s32[128]{0:T(128)}, u32[]{:S(2)}) copy-start(s32[128]{0:T(128)} %param.17) | copy-start | bytes 1540
  14.1 6.4 %copy-start.22 = (s32[128]{0:T(128)S(1)}, s32[128]{0:T(128)}, u32[]{:S(2)}) copy-start(s32[128]{0:T(128)} %param.16) | copy-start | bytes 1540
  20.6 221.0 %copy-start.19 = (s32[128]{0:T(128)}, s32[128]{0:T(128)S(1)}, u32[]{:S(2)}) copy-start(s32[128]{0:T(128)S(1)} %multiply_add_fusion) | copy-start | bytes 1540
  22.5 52.2 %copy-start.14 = (bf16[2,137,512]{2,0,1:T(2,128)(2,1)S(1)}, bf16[2,137,512]{2,0,1:T(2,128)(2,1)}, u32[]{:S(2)}) copy-start(bf16[2,137,512]{2,0,1:T(2,128)(2,1)} %param.11) | copy-start | bytes 841732
  32.7 51.4 %all-to-all-start = ((bf16[16,411,32]{1,2,0:T(8,128)(2,1)}), bf16[16,411,32]{1,2,0:T(8,128)(2,1)S(1)}, u32[]{:S(2)}, u32[]{:S(2)}) async-start(bf16[16,411,32]{1,2,0:T(8,128)(2,1)} %constant_dynamic-update-slice_fusion), calls=%async_computation | async-start | bytes 1048576 | tf_op jit(solution)/shard_map/all_to_all | solution.py:139
  74.9 65.1 %copy-start.15 = (pred[16,8,4]{2,1,0:T(8,128)(4,1)}, pred[16,8,4]{2,1,0:T(8,128)(4,1)S(1)}, u32[]{:S(2)}) copy-start(pred[16,8,4]{2,1,0:T(8,128)(4,1)S(1)} %broadcast_in_dim.137) | copy-start | bytes 1540
  84.1 53.9 %copy-start.17 = (s32[1024]{0:T(1024)}, s32[1024]{0:T(1024)S(1)}, u32[]{:S(2)}) copy-start(s32[1024]{0:T(1024)S(1)} %pad_clamp_fusion) | copy-start | bytes 12292
  84.1 3.7 copy-start.8
  87.9 0.7 copy-start.2
  89.8 8.6 %collective-permute-start = (f32[3,137,192]{2,1,0:T(8,128)}, f32[3,137,192]{2,1,0:T(8,128)}, u32[]{:S(2)}, u32[]{:S(2)}) collective-permute-start(f32[3,137,192]{2,1,0:T(8,128)} %get-tuple-element.539), channel_id=1, source_target_pairs={{1,0},{2,1},{3,2},{4,3},{5,4},{6,5},{7,6},{8,7},{9,8},{10,9},{11,1... | collective-permute-start | bytes 946952 | tf_op jit(solution)/shard_map/while/body/eval_jaxpr/ppermute | solution.py:24
  91.9 11.7 %collective-permute-start.1 = (f32[3,137,192]{2,1,0:T(8,128)S(1)}, f32[3,137,192]{2,1,0:T(8,128)}, u32[]{:S(2)}, u32[]{:S(2)}) collective-permute-start(f32[3,137,192]{2,1,0:T(8,128)S(1)} %get-tuple-element.540), channel_id=1, source_target_pairs={{0,1},{1,2},{2,3},{3,4},{4,5},{5,6},{6,7},{7,8},{8,9},{9,10},{10,1... | collective-permute-start | bytes 946952 | tf_op jit(solution)/shard_map/while/body/eval_jaxpr/ppermute | solution.py:21
  112.2 1.1 copy-start.3
  113.3 0.7 copy-start.2
  115.2 8.6 %collective-permute-start = (f32[3,137,192]{2,1,0:T(8,128)}, f32[3,137,192]{2,1,0:T(8,128)}, u32[]{:S(2)}, u32[]{:S(2)}) collective-permute-start(f32[3,137,192]{2,1,0:T(8,128)} %get-tuple-element.539), channel_id=1, source_target_pairs={{1,0},{2,1},{3,2},{4,3},{5,4},{6,5},{7,6},{8,7},{9,8},{10,9},{11,1... | collective-permute-start | bytes 946952 | tf_op jit(solution)/shard_map/while/body/eval_jaxpr/ppermute | solution.py:24
  115.4 11.7 %collective-permute-start.1 = (f32[3,137,192]{2,1,0:T(8,128)S(1)}, f32[3,137,192]{2,1,0:T(8,128)}, u32[]{:S(2)}, u32[]{:S(2)}) collective-permute-start(f32[3,137,192]{2,1,0:T(8,128)S(1)} %get-tuple-element.540), channel_id=1, source_target_pairs={{0,1},{1,2},{2,3},{3,4},{4,5},{5,6},{6,7},{7,8},{8,9},{9,10},{10,1... | collective-permute-start | bytes 946952 | tf_op jit(solution)/shard_map/while/body/eval_jaxpr/ppermute | solution.py:21
  135.8 1.1 copy-start.3
  136.8 0.7 copy-start.4
  185.2 7.4 %copy-start.11 = (s32[3,128,231]{1,2,0:T(8,128)S(1)}, s32[3,128,231]{1,2,0:T(8,128)}, u32[]{:S(2)}) copy-start(s32[3,128,231]{1,2,0:T(8,128)} %param.15) | copy-start | bytes 1064452
  213.9 20.7 %copy-start.6 = (f32[3,128,231]{1,2,0:T(8,128)}, f32[3,128,231]{1,2,0:T(8,128)S(1)}, u32[]{:S(2)}) copy-start(f32[3,128,231]{1,2,0:T(8,128)S(1)} %get-tuple-element.389) | copy-start | bytes 1064452
  234.4 6.8 %copy-start.9 = (f32[3,128,231]{1,0,2:T(4,128)}, f32[3,128,231]{1,0,2:T(4,128)S(1)}, u32[]{:S(2)}) copy-start(f32[3,128,231]{1,0,2:T(4,128)S(1)} %fusion.190) | copy-start | bytes 1064452
  256.6 16.1 %all-to-all-start.4 = ((bf16[16,822,32]{1,2,0:T(8,128)(2,1)}), bf16[16,822,32]{1,2,0:T(8,128)(2,1)S(1)}, u32[]{:S(2)}, u32[]{:S(2)}) async-start(bf16[16,822,32]{1,2,0:T(8,128)(2,1)} %constant_dynamic-update-slice_fusion.16), calls=%async_computation.4 | async-start | bytes 1835008 | tf_op jit(solution)/shard_map/all_to_all | solution.py:139
  275.8 3.9 copy-start.5
  283.2 13.4 %collective-permute-start.2 = (f32[6,137,192]{2,1,0:T(8,128)}, f32[6,137,192]{2,1,0:T(8,128)}, u32[]{:S(2)}, u32[]{:S(2)}) collective-permute-start(f32[6,137,192]{2,1,0:T(8,128)} %get-tuple-element.558), channel_id=1, source_target_pairs={{1,0},{2,1},{3,2},{4,3},{5,4},{6,5},{7,6},{8,7},{9,8},{10,9},{11,1... | collective-permute-start | bytes 1893896 | tf_op jit(solution)/shard_map/while/body/eval_jaxpr/ppermute | solution.py:24
  284.4 16.5 %collective-permute-start.3 = (f32[6,137,192]{2,1,0:T(8,128)S(1)}, f32[6,137,192]{2,1,0:T(8,128)}, u32[]{:S(2)}, u32[]{:S(2)}) collective-permute-start(f32[6,137,192]{2,1,0:T(8,128)S(1)} %get-tuple-element.559), channel_id=1, source_target_pairs={{0,1},{1,2},{2,3},{3,4},{4,5},{5,6},{6,7},{7,8},{8,9},{9,10},{10,1... | collective-permute-start | bytes 1893896 | tf_op jit(solution)/shard_map/while/body/eval_jaxpr/ppermute | solution.py:21
  314.5 2.4 copy-start
  319.0 1.2 copy-start.1
  323.5 13.4 %collective-permute-start.2 = (f32[6,137,192]{2,1,0:T(8,128)}, f32[6,137,192]{2,1,0:T(8,128)}, u32[]{:S(2)}, u32[]{:S(2)}) collective-permute-start(f32[6,137,192]{2,1,0:T(8,128)} %get-tuple-element.558), channel_id=1, source_target_pairs={{1,0},{2,1},{3,2},{4,3},{5,4},{6,5},{7,6},{8,7},{9,8},{10,9},{11,1... | collective-permute-start | bytes 1893896 | tf_op jit(solution)/shard_map/while/body/eval_jaxpr/ppermute | solution.py:24
  323.7 16.5 %collective-permute-start.3 = (f32[6,137,192]{2,1,0:T(8,128)S(1)}, f32[6,137,192]{2,1,0:T(8,128)}, u32[]{:S(2)}, u32[]{:S(2)}) collective-permute-start(f32[6,137,192]{2,1,0:T(8,128)S(1)} %get-tuple-element.559), channel_id=1, source_target_pairs={{0,1},{1,2},{2,3},{3,4},{4,5},{5,6},{6,7},{7,8},{8,9},{9,10},{10,1... | collective-permute-start | bytes 1893896 | tf_op jit(solution)/shard_map/while/body/eval_jaxpr/ppermute | solution.py:21
  353.8 2.4 copy-start
  358.3 1.2 copy-start.1
  361.4 0.8 copy-start.18
  364.9 1.9 copy-start.16
  422.5 0.8 copy-start.20
  429.2 1.0 copy-start.7
  429.2 1.1 copy-start.10
  429.2 1.2 copy-start.12
